TPU v7x, 32 devices: a whole 2x2x4 slice. The times are simulated.
32 devices in a mesh: groups: 2 (over x), worker: 2 (over core), tensor: 8 (over z, y).
Axes of the slice: x: 2, y: 2, z: 4, core: 2. Of those that a mesh axis runs over, the one named last changes fastest.
Arguments:
- tokens: bfloat16 [1024, 8192], P(('groups', 'worker'), 'tensor'), parts along dimension 0, may hold values from -6 to 6
- norm_gain: float32 [8192], replicated, may hold values from 0.5 to 1.5
- query_weight: bfloat16 [8192, 8192], P(None, 'tensor'), may hold values from -0.0625 to 0.0625
- key_weight: bfloat16 [8192, 1024], P(None, 'tensor'), may hold values from -0.15625 to 0.15625
- value_weight: bfloat16 [8192, 1024], P(None, 'tensor'), may hold values from -0.0625 to 0.0625
- output_weight: bfloat16 [8192, 8192], P('tensor'), may hold values from -0.0625 to 0.0625
- cached_blocks: bfloat16 [8, 1024, 2, 1024], P(('groups', 'worker'), 'tensor'), parts along dimension 0
- cache_length: int32 [8], P('groups'), parts along dimension 0, may hold values from 256 to 1024, as said below
- block_table: int32 [8, 64], P('groups'), parts along dimension 0, may hold values from 0 to 63, each once within a row
- destination: int32 [8], P('groups'), parts along dimension 0, may hold values from 0 to 1, as said below
Outputs:
- attended: bfloat16 [4, 3, 128, 8192], P(('groups', 'worker'), None, None, 'tensor'), parts along dimension 0
There are 2 independent parts, one for each index of `groups`. A program takes and returns all parts, laid end to end along the dimension named above; an argument that names none is the same for every part. Nothing has to cross between parts.
Inputs may be any that keep to these rules, and one draw needn't show every extreme that they name: Exactly 3 sequences have one destination, the others the other; which one is drawn. `cache_length`: some sequence has exactly 1024 cached tokens.
All inputs are finite; a program needn't handle non-finite values.
Results may differ from a plain program's by a relative error of at most 0.02.
The roundings to bfloat16 on the way count: a program that leaves them out, or rounds other values in their place, can miss the bound.
Values may be sent and summed in bfloat16 or wider, within the bound.
No kernel may reach another device: no remote copies, remote signals or barrier semaphores. Data moves between devices by JAX's collectives and lax.ppermute only.
A program may use at most 128 MiB of HBM per device.

v0:
```python
import math
import jax
import jax.numpy as jnp
from jax import lax
from jax.sharding import PartitionSpec as P

D = 8192
KVH = 8
HD = 128
NEW = 128
BLK = 16
CAP = 3
epsilon = 1e-05


def from_partner(block, axis, bit):
    count = lax.axis_size(axis)
    route = []
    for low in range(count):
        high = low | 1 << bit
        if high != low and high < count:
            route += [(low, high), (high, low)]
    return lax.ppermute(block, axis, route)


def rotate(values, positions):
    halfway = HD // 2
    inverse = 500000.0 ** (-(jnp.arange(halfway, dtype=jnp.float32) * 2.0 / HD))
    angles = positions[:, None] * inverse[None, :]
    cosine_table = jnp.concatenate([jnp.cos(angles), jnp.cos(angles)], axis=-1)[:, None, :]
    sine_table = jnp.concatenate([jnp.sin(angles), jnp.sin(angles)], axis=-1)[:, None, :]
    turned = jnp.concatenate([-values[..., halfway:], values[..., :halfway]], axis=-1)
    return values * cosine_table + turned * sine_table


def attend(
    token_rows,
    blocks,
    lengths,
    tables,
    norm_gain,
    query_weight,
    key_weight,
    value_weight,
    output_weight,
):
    tensor_count = lax.axis_size("tensor")
    tensor_index = lax.axis_index("tensor")
    group_width = tensor_count // KVH
    bit_count = group_width.bit_length() - 1
    seq_count = blocks.shape[0]
    total = token_rows.shape[0]
    query_cols = query_weight.shape[1]
    widened = lax.all_gather(token_rows, "tensor", axis=1, tiled=True).astype(jnp.float32)
    scaled = (widened * norm_gain[None, :]).astype(jnp.bfloat16)
    query_sum = jnp.dot(scaled, query_weight, preferred_element_type=jnp.float32)
    key_sum = jnp.dot(scaled, key_weight, preferred_element_type=jnp.float32)
    value_sum = jnp.dot(scaled, value_weight, preferred_element_type=jnp.float32)
    squares = jnp.sum(widened * widened, axis=1)
    factor = lax.rsqrt(squares / D + epsilon)[:, None]
    positions = (
        (lengths[:, None] + jnp.arange(NEW, dtype=jnp.int32)[None, :])
        .reshape(total)
        .astype(jnp.float32)
    )
    heads_here = query_cols // HD
    queries = rotate((query_sum * factor).reshape(total, heads_here, HD), positions).astype(
        jnp.bfloat16
    )
    key_full = (key_sum * factor).astype(jnp.bfloat16)
    value_full = (value_sum * factor).astype(jnp.bfloat16)
    for bit in range(bit_count):
        other_key, other_value = from_partner((key_full, value_full), "tensor", bit)
        upper = tensor_index // (1 << bit) % 2 == 1
        key_full = jnp.where(
            upper,
            jnp.concatenate([other_key, key_full], axis=1),
            jnp.concatenate([key_full, other_key], axis=1),
        )
        value_full = jnp.where(
            upper,
            jnp.concatenate([other_value, value_full], axis=1),
            jnp.concatenate([value_full, other_value], axis=1),
        )
    new_key = rotate(key_full.astype(jnp.float32)[:, None, :], positions)[:, 0, :].astype(
        jnp.bfloat16
    )
    fresh_keys = new_key.reshape(seq_count, NEW, HD)
    fresh_values = value_full.reshape(seq_count, NEW, HD)
    local_tokens = blocks.shape[1]
    inverse_root = 1.0 / math.sqrt(HD)
    query_blocks = queries.reshape(seq_count, NEW, heads_here, HD)
    causal = jnp.arange(NEW)[:, None] >= jnp.arange(NEW)[None, :]
    spread = jnp.repeat(
        blocks.reshape(seq_count, local_tokens, 2, KVH, HD), tensor_count // KVH, axis=3
    )
    arrived = lax.all_to_all(spread, "tensor", split_axis=3, concat_axis=1, tiled=True)
    context = arrived.shape[1]
    old_key = arrived[:, :, 0, 0, :]
    old_value = arrived[:, :, 1, 0, :]
    stored = jnp.arange(context, dtype=jnp.int32)
    logical = jnp.take(tables, stored // BLK, axis=1) * BLK + stored % BLK
    visible = logical < lengths[:, None]
    old_scores = (
        jnp.einsum("sqhd,skd->shqk", query_blocks, old_key, preferred_element_type=jnp.float32)
        * inverse_root
    )
    old_scores = jnp.where(visible[:, None, None, :], old_scores, -1e30)
    new_scores = (
        jnp.einsum("sqhd,skd->shqk", query_blocks, fresh_keys, preferred_element_type=jnp.float32)
        * inverse_root
    )
    new_scores = jnp.where(causal[None, None], new_scores, -1e30)
    largest = jnp.maximum(jnp.max(old_scores, axis=3), jnp.max(new_scores, axis=3))[..., None]
    old_expo = jnp.exp(old_scores - largest)
    new_expo = jnp.exp(new_scores - largest)
    denominator = (jnp.sum(old_expo, axis=3) + jnp.sum(new_expo, axis=3))[..., None]
    old_probs = (old_expo / denominator).astype(jnp.bfloat16)
    new_probs = (new_expo / denominator).astype(jnp.bfloat16)
    mixture = jnp.einsum("shqk,skd->sqhd", old_probs, old_value, preferred_element_type=jnp.float32)
    mixture = mixture + jnp.einsum(
        "shqk,skd->sqhd", new_probs, fresh_values, preferred_element_type=jnp.float32
    )
    attended_rows = mixture.astype(jnp.bfloat16).reshape(total, heads_here * HD)
    partial_value = jnp.dot(attended_rows, output_weight, preferred_element_type=jnp.float32)
    summed = lax.psum_scatter(partial_value, "tensor", scatter_dimension=1, tiled=True)
    return summed.astype(jnp.bfloat16)


def local(
    tokens,
    norm_gain,
    query_weight,
    key_weight,
    value_weight,
    output_weight,
    cached_blocks,
    cache_length,
    block_table,
    destination,
):
    worker_index = lax.axis_index("worker")
    seq_total = destination.shape[0]
    belongs = (destination == worker_index).astype(jnp.int32)
    ranking = jnp.cumsum(belongs) - 1
    matched = (belongs[None, :] == 1) & (
        ranking[None, :] == jnp.arange(CAP, dtype=jnp.int32)[:, None]
    )
    slot_owner = jnp.sum(
        matched.astype(jnp.int32) * jnp.arange(seq_total, dtype=jnp.int32)[None, :], axis=1
    )
    occupied = jnp.any(matched, axis=1)
    local_count = cached_blocks.shape[0]
    owned = worker_index * local_count + jnp.arange(local_count, dtype=jnp.int32)
    mixed = attend(
        tokens,
        cached_blocks,
        jnp.take(cache_length, owned),
        jnp.take(block_table, owned, axis=0),
        norm_gain,
        query_weight,
        key_weight,
        value_weight,
        output_weight,
    )
    everyone = lax.all_gather(mixed, "worker", axis=0, tiled=True)
    placed = jnp.take(everyone.reshape(seq_total, NEW, -1), slot_owner, axis=0)
    result = jnp.where(occupied[:, None, None], placed, jnp.zeros_like(placed))
    return result[None]


def solution(mesh):
    placed = (
        P(("groups", "worker"), "tensor"),
        P(),
        P(None, "tensor"),
        P(None, "tensor"),
        P(None, "tensor"),
        P("tensor", None),
        P(("groups", "worker"), "tensor", None, None),
        P("groups"),
        P("groups", None),
        P("groups"),
    )
    return jax.shard_map(
        local,
        mesh=mesh,
        in_specs=placed,
        out_specs=P(("groups", "worker"), None, None, "tensor"),
        check_vma=False,
    )
```

profile of v0, /device:TPU:0, one launch (start us, length us, event | category | flops | bytes accessed | tf_op | source)
XLA Modules:
  0.0 310.5 jit_solution(4129475814052174620)
XLA Ops:
  6.5 0.0 copy-start
  6.5 0.0 all-gather.3.cloned.1.call-start
  6.5 0.7 all-gather.3.cloned.1.call-update
  7.3 2.6 copy.86
  9.8 1.3 copy.87
  11.1 7.3 %all-to-all-start = ((bf16[2,128,2,8,128]{4,1,0,2,3:T(8,128)(2,1)}), bf16[2,128,2,8,128]{4,1,0,2,3:T(8,128)(2,1)S(1)}, u32[]{:S(2)}, u32[]{:S(2)}) async-start(bf16[2,128,2,8,128]{4,1,0,2,3:T(8,128)(2,1)} %copy.87), calls=%async_computation | async-start | bytes 2097152 | tf_op jit(solution)/shard_map/all_to_all | solution.py:97
  18.4 0.0 reduce-scatter.2.cloned.1.call-start
  18.5 1.3 gather_fusion.2
  19.8 1.3 gather_fusion
  21.1 0.1 broadcast_select_fusion
  21.2 0.1 copy.80
  21.3 4.0 %gather_fusion.1 = s32[1024,2]{1,0:T(8,128)} fusion(s32[2,64]{0,1:T(8,128)S(1)} %copy.80, s32[1024]{0:T(1024)S(1)} %broadcast_clamp_fusion), kind=kCustom, calls=%fused_computation.1 | custom fusion | bytes 20480 | tf_op jit(solution)/shard_map/jit(_take)/gather | solution.py:102
  25.3 1.2 copy.81
  26.6 0.6 iota_compare_fusion
  27.2 0.1 fusion.68
  27.3 0.5 multiply_cosine_fusion
  27.8 0.1 pad_maximum_fusion
  28.0 0.1 compare_bitcast_fusion
  28.0 0.3 multiply_sine_fusion.1
  28.3 32.7 %all-to-all-done = bf16[2,128,2,8,128]{4,1,0,2,3:T(8,128)(2,1)S(1)} async-done(((bf16[2,128,2,8,128]{4,1,0,2,3:T(8,128)(2,1)}), bf16[2,128,2,8,128]{4,1,0,2,3:T(8,128)(2,1)S(1)}, u32[]{:S(2)}, u32[]{:S(2)}) %all-to-all-start) | async-done | bytes 1048608 | tf_op jit(solution)/shard_map/all_to_all | solution.py:97
  61.1 1.0 copy.88
  62.1 40.3 %all-gather.3.cloned.1.call-done = bf16[256,8192]{1,0:T(8,128)(2,1)} async-done(((bf16[256,1024]{1,0:T(8,128)(2,1)}), bf16[256,8192]{1,0:T(8,128)(2,1)}) %all-gather.3.cloned.1.call-update) | async-done | bytes 4194320 | tf_op jit(solution)/shard_map/all_gather | solution.py:54
  102.4 3.1 fusion.1
  105.5 0.0 copy-done
  105.5 3.6 %fusion.25 = bf16[256,128]{0,1:T(8,128)(2,1)S(1)} fusion(bf16[8192,128]{1,0:T(8,128)(2,1)S(1)} %copy-done, bf16[256,8192]{1,0:T(8,128)(2,1)} %all-gather.3.cloned.1.call-done, f32[8192]{0:T(1024)} %param.11, f32[256]{0:T(256)S(1)} %add_rsqrt_fusion), kind=kOutput, calls=%fused_computation.28 | convolution fusion | flops 543227904 | bytes 6390784 | tf_op jit(solution)/shard_map/dot_general | solution.py:58
  109.1 0.6 reshape.302
  109.7 0.0 copy-done.6
  109.7 4.3 %fusion.31 = f32[256,128]{0,1:T(8,128)S(1)} fusion(bf16[8192,128]{1,0:T(8,128)(2,1)} %param.13, bf16[256,8192]{1,0:T(8,128)(2,1)} %all-gather.3.cloned.1.call-done, f32[8192]{0:T(1024)S(1)} %copy-done.6, f32[256]{0:T(256)S(1)} %add_rsqrt_fusion), kind=kOutput, calls=%fused_computation.30 | convolution fusion | flops 543260672 | bytes 6456320 | tf_op jit(solution)/shard_map/dot_general | solution.py:57
  114.1 0.1 copy.106
  114.2 9.5 %fusion.11 = f32[256,1024]{1,0:T(8,128)S(1)} fusion(bf16[8192,1024]{1,0:T(8,128)(2,1)} %param.12, bf16[256,8192]{1,0:T(8,128)(2,1)} %all-gather.3.cloned.1.call-done, f32[8192]{0:T(1024)} %param.11, f32[256]{0:T(256)S(1)} %add_rsqrt_fusion), kind=kOutput, calls=%fused_computation.18 | convolution fusion | flops 4301520896 | bytes 22053888 | tf_op jit(solution)/shard_map/dot_general | solution.py:56
  123.8 0.3 copy.109
  124.1 0.2 copy.110
  124.3 0.9 slice_negate_fusion
  125.2 0.4 copy.104
  125.6 1.5 copy.105
  127.1 0.4 fusion.35
  127.5 0.3 fusion.69
  127.8 0.0 copy-start.2
  127.8 2.6 bitcast_reduce_fusion
  130.5 0.2 fusion.36
  130.6 0.0 slice-start
  130.6 2.1 fusion.3
  132.8 0.0 slice-start.1
  132.8 0.0 slice-start.2
  132.8 0.0 slice-start.3
  132.8 2.5 fusion.17
  135.3 0.4 fusion.18
  135.7 0.3 copy.96
  136.1 0.1 slice-done.2
  136.2 1.2 slice-done.3
  137.4 6.7 %fusion.38 = f32[256,8192]{1,0:T(8,128)} fusion(bf16[1024,8192]{1,0:T(8,128)(2,1)S(1)} %bitcast.101, bf16[32,8,8,128]{3,2,1,0:T(8,128)(2,1)S(1)} %bitcast.109), kind=kOutput, calls=%fused_computation.40 | convolution fusion | flops 4294967296 | bytes 25690112 | tf_op jit(solution)/shard_map/dot_general | solution.py:125
  144.1 0.0 reduce-scatter.2.cloned.1.call-update
  144.2 0.0 all-gather.5.cloned.1.call-start
  144.2 146.5 %reduce-scatter.2.cloned.1.call-done = f32[256,1024]{1,0:T(8,128)} async-done(((f32[256,8192]{1,0:T(8,128)}), f32[256,1024]{1,0:T(8,128)}) %reduce-scatter.2.cloned.1.call-update) | async-done | bytes 1048592 | tf_op jit(solution)/shard_map/reduce_scatter | solution.py:126
  290.7 2.1 convert_element_type.67
  292.8 0.0 all-gather.5.cloned.1.call-update
  292.8 0.0 copy-done.5
  292.8 0.2 reduce-window.8
  293.0 0.1 select_reduce_fusion
  293.2 0.1 fusion.61
  293.3 7.8 %all-gather.5.cloned.1.call-done = bf16[512,1024]{1,0:T(8,128)(2,1)} async-done(((bf16[256,1024]{1,0:T(8,128)(2,1)}), bf16[512,1024]{1,0:T(8,128)(2,1)}) %all-gather.5.cloned.1.call-update) | async-done | bytes 1048592 | tf_op jit(solution)/shard_map/all_gather | solution.py:166
  301.1 1.8 gather_fusion.3
  302.9 1.0 fusion.37
  304.0 0.0 copy-done.1
  (30 shorter events, 0.2 us)
Async XLA Ops:
  6.5 98.9 %copy-start = (bf16[8192,128]{1,0:T(8,128)(2,1)S(1)}, bf16[8192,128]{1,0:T(8,128)(2,1)}, u32[]{:S(2)}) copy-start(bf16[8192,128]{1,0:T(8,128)(2,1)} %param.14) | copy-start | bytes 6291460
  6.5 95.8 %all-gather.3.cloned.1.call-start = ((), (), s32[]{:S(2)}) async-start(), calls=%async_computation.2 | async-start | bytes 4718592 | tf_op jit(solution)/shard_map/all_gather | solution.py:54
  11.1 49.9 %all-to-all-start = ((bf16[2,128,2,8,128]{4,1,0,2,3:T(8,128)(2,1)}), bf16[2,128,2,8,128]{4,1,0,2,3:T(8,128)(2,1)S(1)}, u32[]{:S(2)}, u32[]{:S(2)}) async-start(bf16[2,128,2,8,128]{4,1,0,2,3:T(8,128)(2,1)} %copy.87), calls=%async_computation | async-start | bytes 2097152 | tf_op jit(solution)/shard_map/all_to_all | solution.py:97
  18.4 272.2 %reduce-scatter.2.cloned.1.call-start = ((), (), s32[]{:S(2)}) async-start(), calls=%async_computation.3 | async-start | bytes 9437184 | tf_op jit(solution)/shard_map/reduce_scatter | solution.py:126
  62.1 47.6 %copy-start.6 = (f32[8192]{0:T(1024)S(1)}, f32[8192]{0:T(1024)}, u32[]{:S(2)}) copy-start(f32[8192]{0:T(1024)} %param.11) | copy-start | bytes 98308
  123.8 3.7 %copy-start.3 = (pred[128,128]{0,1:T(8,128)(4,1)S(1)}, pred[128,128]{0,1:T(8,128)(4,1)}, u32[]{:S(2)}) copy-start(pred[128,128]{0,1:T(8,128)(4,1)} %iota_compare_fusion) | copy-start | bytes 49156
  127.8 4.9 %copy-start.2 = (bf16[2,8,128,2,1,128]{5,2,1,0,3,4:T(8,128)(2,1)S(1)}, bf16[2,8,128,2,1,128]{5,2,1,0,3,4:T(8,128)(2,1)}, u32[]{:S(2)}) copy-start(bf16[2,8,128,2,1,128]{5,2,1,0,3,4:T(8,128)(2,1)} %copy.88) | copy-start | bytes 3145732
  130.6 5.4 %slice-start = ((s8[16777216]{0:T(1024)(128)(4,1)}), s8[4194304]{0:T(1024)(128)(4,1)S(1)}, s32[]{:S(2)}) async-start(s8[16777216]{0:T(1024)(128)(4,1)} %bitcast.100), calls=%async_computation.5 | async-start | bytes 8388608
  132.8 2.5 copy-start.4
  132.8 3.3 %slice-start.1 = ((s8[16777216]{0:T(1024)(128)(4,1)}), s8[4194304]{0:T(1024)(128)(4,1)S(1)}, s32[]{:S(2)}) async-start(s8[16777216]{0:T(1024)(128)(4,1)} %bitcast.100), calls=%async_computation.6 | async-start | bytes 8388608
  132.8 3.4 %slice-start.2 = ((s8[16777216]{0:T(1024)(128)(4,1)}), s8[4194304]{0:T(1024)(128)(4,1)S(1)}, s32[]{:S(2)}) async-start(s8[16777216]{0:T(1024)(128)(4,1)} %bitcast.100), calls=%async_computation.7 | async-start | bytes 8388608
  132.8 4.6 %slice-start.3 = ((s8[16777216]{0:T(1024)(128)(4,1)}), s8[4194304]{0:T(1024)(128)(4,1)S(1)}, s32[]{:S(2)}) async-start(s8[16777216]{0:T(1024)(128)(4,1)} %bitcast.100), calls=%async_computation.8 | async-start | bytes 8388608
  137.4 166.6 %copy-start.1 = (bf16[8192,128]{1,0:T(8,128)(2,1)S(1)}, bf16[8192,128]{1,0:T(8,128)(2,1)}, u32[]{:S(2)}) copy-start(bf16[8192,128]{1,0:T(8,128)(2,1)} %param.14) | copy-start | bytes 6291460
  144.1 148.7 %copy-start.5 = (s32[4]{0:T(128)S(1)}, s32[4]{0:T(128)}, u32[]{:S(2)}) copy-start(s32[4]{0:T(128)} %param.19) | copy-start | bytes 52
  144.2 156.9 %all-gather.5.cloned.1.call-start = ((), (), s32[]{:S(2)}) async-start(), calls=%async_computation.4 | async-start | bytes 1572864 | tf_op jit(solution)/shard_map/all_gather | solution.py:166
Sparse Core Ops, SparseCore 0:
  9.5 92.8 all-gather.2
  144.3 146.3 reduce-scatter.1
  292.9 8.1 all-gather.4
where the time goes:
time: 311 us; the launch traced here: 310 us
  waiting for transfers between devices  228 us (73%)
  matrix products  30 us (10%)
  local copies, waits for them, and re-layouts  19.5 us (6%)
  between operations  13.5 us (4%)
  other arithmetic  12.2 us (4%)
  starting transfers between devices  7.39 us (2%)
    reduce_scatter x1, waiting for transfers between devices, attend(): lax.psum_scatter(partial_value, 'tensor', scatter_dimension=1, tiled=True)  146 us
    all_gather x1, waiting for transfers between devices, attend(): lax.all_gather(token_rows, 'tensor', axis=1, tiled=True).astype(jnp.float32)  40.3 us
    all_to_all x1, waiting for transfers between devices, attend(): lax.all_to_all(spread, 'tensor', split_axis=3, concat_axis=1, tiled=True)  32.7 us
    dot_general x1, matrix products, attend(): jnp.dot(scaled, query_weight, preferred_element_type=jnp.float32)  9.52 us
    all_gather x1, waiting for transfers between devices, local(): everyone = lax.all_gather(mixed, 'worker', axis=0, tiled=True)  7.81 us
    all_to_all x1, starting transfers between devices, attend(): lax.all_to_all(spread, 'tensor', split_axis=3, concat_axis=1, tiled=True)  7.31 us
    dot_general x1, matrix products, attend(): jnp.dot(attended_rows, output_weight, preferred_element_type=jnp.float32)  6.74 us
  transfers between devices with their start and end apart: 4, of which 4 were waited for; matrix products, arithmetic and copies ran while one was open for 5% of the time, Pallas kernels for 0%

commit v1 on v0

--- a/solution.py
+++ b/solution.py
@@ -11,6 +11,13 @@
 BLK = 16
 CAP = 3
 epsilon = 1e-05
+
+
+def swapped_in(value, name, dim):
+    size = lax.axis_size(name)
+    tiles = jnp.stack([value for _ in range(size)])
+    tiles = lax.all_to_all(tiles, name, split_axis=0, concat_axis=0)
+    return jnp.concatenate(tiles, axis=dim)
 
 
 def from_partner(block, axis, bit):
@@ -51,7 +58,7 @@
     seq_count = blocks.shape[0]
     total = token_rows.shape[0]
     query_cols = query_weight.shape[1]
-    widened = lax.all_gather(token_rows, "tensor", axis=1, tiled=True).astype(jnp.float32)
+    widened = swapped_in(token_rows, "tensor", 1).astype(jnp.float32)
     scaled = (widened * norm_gain[None, :]).astype(jnp.bfloat16)
     query_sum = jnp.dot(scaled, query_weight, preferred_element_type=jnp.float32)
     key_sum = jnp.dot(scaled, key_weight, preferred_element_type=jnp.float32)

time: 311 us -> 359 us (1.15)
  waiting for transfers between devices: 228 us -> 261 us
  local copies, waits for them, and re-layouts: 19.5 us -> 27.6 us
  starting transfers between devices: 7.39 us -> 12.1 us
  other arithmetic: 12.2 us -> 16.6 us
    all_to_all x0 -> x1, waiting for transfers between devices: none -> 82.8 us  [swapped_in(): tiles = lax.all_to_all(tiles, name, split_axis=0, concat_axis=0)]
    all_gather x1 -> x0, waiting for transfers between devices: 40.3 us -> none  [attend(): lax.all_gather(token_rows, 'tensor', axis=1, tiled=True).astype(jnp.float32)]
    all_to_all x1, waiting for transfers between devices: 32.7 us -> 23.7 us  [attend(): lax.all_to_all(spread, 'tensor', split_axis=3, concat_axis=1, tiled=True)]
    all_to_all x0 -> x1, starting transfers between devices: none -> 4.55 us  [swapped_in(): tiles = lax.all_to_all(tiles, name, split_axis=0, concat_axis=0)]
    unnamed x24 -> x29, local copies, waits for them, and re-layouts: 4.12 us -> 8.31 us
  transfers between devices with their start and end apart: 4 -> 4, of which waited for: 4 -> 4; matrix products, arithmetic and copies ran while one was open for 5% -> 3% of each run, Pallas kernels for 0% -> 0%
where the time goes in v1:
time: 359 us; the launch traced here: 358 us
  waiting for transfers between devices  261 us (73%)
  local copies, waits for them, and re-layouts  27.6 us (8%)
  matrix products  26.5 us (7%)
  other arithmetic  16.6 us (5%)
  between operations  13.8 us (4%)
  starting transfers between devices  12.1 us (3%)
    reduce_scatter x1, waiting for transfers between devices, attend(): lax.psum_scatter(partial_value, 'tensor', scatter_dimension=1, tiled=True)  147 us
    all_to_all x1, waiting for transfers between devices, swapped_in(): tiles = lax.all_to_all(tiles, name, split_axis=0, concat_axis=0)  82.8 us
    all_to_all x1, waiting for transfers between devices, attend(): lax.all_to_all(spread, 'tensor', split_axis=3, concat_axis=1, tiled=True)  23.7 us
    unnamed x29, local copies, waits for them, and re-layouts  8.31 us
    dot_general x1, matrix products, attend(): jnp.dot(scaled, query_weight, preferred_element_type=jnp.float32)  8.27 us
    all_gather x1, waiting for transfers between devices, local(): everyone = lax.all_gather(mixed, 'worker', axis=0, tiled=True)  7.79 us
    all_to_all x1, starting transfers between devices, attend(): lax.all_to_all(spread, 'tensor', split_axis=3, concat_axis=1, tiled=True)  7.44 us
  transfers between devices with their start and end apart: 4, of which 4 were waited for; matrix products, arithmetic and copies ran while one was open for 3% of the time, Pallas kernels for 0%

profile of v1, /device:TPU:0, one launch (start us, length us, event | category | flops | bytes accessed | tf_op | source)
XLA Modules:
  0.0 358.0 jit_solution(5096807249290649992)
XLA Ops:
  6.5 2.7 copy.91
  9.2 1.3 copy.92
  10.5 7.4 %all-to-all-start.1 = ((bf16[2,128,2,8,128]{4,1,0,2,3:T(8,128)(2,1)}), bf16[2,128,2,8,128]{4,1,0,2,3:T(8,128)(2,1)S(1)}, u32[]{:S(2)}, u32[]{:S(2)}) async-start(bf16[2,128,2,8,128]{4,1,0,2,3:T(8,128)(2,1)} %copy.92), calls=%async_computation.1 | async-start | bytes 2097152 | tf_op jit(solution)/shard_map/all_to_all | solution.py:104
  18.0 2.0 copy.86
  20.0 23.7 %all-to-all-done.1 = bf16[2,128,2,8,128]{4,1,0,2,3:T(8,128)(2,1)S(1)} async-done(((bf16[2,128,2,8,128]{4,1,0,2,3:T(8,128)(2,1)}), bf16[2,128,2,8,128]{4,1,0,2,3:T(8,128)(2,1)S(1)}, u32[]{:S(2)}, u32[]{:S(2)}) %all-to-all-start.1) | async-done | bytes 1048608 | tf_op jit(solution)/shard_map/all_to_all | solution.py:104
  43.8 3.3 stack.2
  47.0 4.6 %all-to-all-start = ((bf16[8,256,1024]{1,2,0:T(8,128)(2,1)}), bf16[8,256,1024]{1,2,0:T(8,128)(2,1)}, u32[]{:S(2)}, u32[]{:S(2)}) async-start(bf16[8,256,1024]{1,2,0:T(8,128)(2,1)} %stack.2), calls=%async_computation | async-start | bytes 8388608 | tf_op jit(solution)/shard_map/all_to_all | solution.py:19
  51.6 0.0 reduce-scatter.2.cloned.1.call-start
  51.7 0.6 gather_fusion.2
  52.3 0.6 gather_fusion
  52.9 0.1 broadcast_select_fusion
  53.0 0.1 copy.84
  53.1 4.0 %gather_fusion.1 = s32[1024,2]{1,0:T(8,128)} fusion(s32[2,64]{0,1:T(8,128)S(1)} %copy.84, s32[1024]{0:T(1024)S(1)} %broadcast_clamp_fusion), kind=kCustom, calls=%fused_computation.1 | custom fusion | bytes 20480 | tf_op jit(solution)/shard_map/jit(_take)/gather | solution.py:109
  57.1 1.2 copy.85
  58.4 0.6 iota_compare_fusion
  59.0 0.1 fusion.46
  59.1 0.5 multiply_cosine_fusion
  59.6 0.1 pad_maximum_fusion
  59.8 0.1 compare_bitcast_fusion
  59.9 0.3 multiply_sine_fusion.1
  60.2 1.1 copy.93
  61.3 82.8 %all-to-all-done = bf16[8,256,1024]{1,2,0:T(8,128)(2,1)} async-done(((bf16[8,256,1024]{1,2,0:T(8,128)(2,1)}), bf16[8,256,1024]{1,2,0:T(8,128)(2,1)}, u32[]{:S(2)}, u32[]{:S(2)}) %all-to-all-start) | async-done | bytes 4194336 | tf_op jit(solution)/shard_map/all_to_all | solution.py:19
  144.1 3.3 multiply_reduce_fusion
  147.4 2.9 fusion
  150.3 1.9 copy-done.3
  152.3 1.0 fusion.11
  153.3 0.6 reshape.308
  154.0 4.0 %fusion.10 = f32[256,128]{0,1:T(8,128)S(1)} fusion(bf16[256,8192]{0,1:T(8,128)(2,1)} %copy-done.3, bf16[8192,128]{1,0:T(8,128)(2,1)} %param.13, f32[256]{0:T(256)S(1)} %add_rsqrt_fusion), kind=kOutput, calls=%fused_computation.25 | convolution fusion | flops 536969216 | bytes 6423552 | tf_op jit(solution)/shard_map/dot_general | solution.py:64
  157.9 0.1 copy-done.4
  158.0 8.3 %convolution_multiply_fusion = f32[256,1024]{1,0:T(8,128)S(1)} fusion(bf16[256,8192]{0,1:T(8,128)(2,1)S(1)} %copy-done.4, bf16[8192,1024]{1,0:T(8,128)(2,1)} %param.12, f32[256]{0:T(256)S(1)} %add_rsqrt_fusion), kind=kOutput, calls=%fused_computation.14 | convolution fusion | flops 4295229440 | bytes 22021120 | tf_op jit(solution)/shard_map/dot_general | solution.py:63
  166.3 0.1 copy.111
  166.5 0.3 copy.114
  166.8 0.2 copy.115
  167.0 1.1 slice_negate_fusion
  168.1 1.5 copy.109
  169.6 2.4 copy.110
  171.9 1.6 fusion.13
  173.5 1.0 fusion.47
  174.5 2.6 bitcast_reduce_fusion
  177.2 0.2 fusion.14
  177.3 0.0 slice-start
  177.3 2.1 fusion.2
  179.5 0.0 copy-done.5
  179.5 0.0 copy-start.6
  179.5 0.0 slice-start.1
  179.5 0.0 slice-start.2
  179.5 0.0 slice-start.3
  179.5 2.5 fusion.7
  182.0 0.4 fusion.8
  182.4 0.3 copy.101
  182.8 0.1 slice-done.2
  182.9 1.2 slice-done.3
  184.1 6.8 %fusion.16 = f32[256,8192]{1,0:T(8,128)} fusion(bf16[1024,8192]{1,0:T(8,128)(2,1)S(1)} %bitcast.110, bf16[32,8,8,128]{3,2,1,0:T(8,128)(2,1)S(1)} %bitcast.118), kind=kOutput, calls=%fused_computation.36 | convolution fusion | flops 4294967296 | bytes 25690112 | tf_op jit(solution)/shard_map/dot_general | solution.py:132
  190.8 0.0 reduce-scatter.2.cloned.1.call-update
  190.9 0.0 all-gather.2.cloned.1.call-start
  190.9 147.0 %reduce-scatter.2.cloned.1.call-done = f32[256,1024]{1,0:T(8,128)} async-done(((f32[256,8192]{1,0:T(8,128)}), f32[256,1024]{1,0:T(8,128)}) %reduce-scatter.2.cloned.1.call-update) | async-done | bytes 1048592 | tf_op jit(solution)/shard_map/reduce_scatter | solution.py:133
  337.9 2.1 convert_element_type.80
  340.0 0.0 all-gather.2.cloned.1.call-update
  340.1 0.2 reduce-window.8
  340.3 0.1 select_reduce_fusion
  340.4 0.1 fusion.39
  340.5 7.8 %all-gather.2.cloned.1.call-done = bf16[512,1024]{1,0:T(8,128)(2,1)} async-done(((bf16[256,1024]{1,0:T(8,128)(2,1)}), bf16[512,1024]{1,0:T(8,128)(2,1)}) %all-gather.2.cloned.1.call-update) | async-done | bytes 1048592 | tf_op jit(solution)/shard_map/all_gather | solution.py:173
  348.3 1.8 gather_fusion.3
  350.2 1.0 fusion.15
  (36 shorter events, 0.2 us)
Async XLA Ops:
  6.5 145.7 %copy-start = (bf16[8192,128]{1,0:T(8,128)(2,1)S(1)}, bf16[8192,128]{1,0:T(8,128)(2,1)}, u32[]{:S(2)}) copy-start(bf16[8192,128]{1,0:T(8,128)(2,1)} %param.14) | copy-start | bytes 6291460
  10.5 41.1 %copy-start.2 = (s32[4]{0:T(128)S(1)}, s32[4]{0:T(128)}, u32[]{:S(2)}) copy-start(s32[4]{0:T(128)} %param.17) | copy-start | bytes 52
  10.5 41.8 %copy-start.7 = (s32[4,64]{1,0:T(4,128)S(1)}, s32[4,64]{1,0:T(4,128)}, u32[]{:S(2)}) copy-start(s32[4,64]{1,0:T(4,128)} %param.18) | copy-start | bytes 3076
  10.5 33.2 %all-to-all-start.1 = ((bf16[2,128,2,8,128]{4,1,0,2,3:T(8,128)(2,1)}), bf16[2,128,2,8,128]{4,1,0,2,3:T(8,128)(2,1)S(1)}, u32[]{:S(2)}, u32[]{:S(2)}) async-start(bf16[2,128,2,8,128]{4,1,0,2,3:T(8,128)(2,1)} %copy.92), calls=%async_computation.1 | async-start | bytes 2097152 | tf_op jit(solution)/shard_map/all_to_all | solution.py:104
  47.0 97.1 %all-to-all-start = ((bf16[8,256,1024]{1,2,0:T(8,128)(2,1)}), bf16[8,256,1024]{1,2,0:T(8,128)(2,1)}, u32[]{:S(2)}, u32[]{:S(2)}) async-start(bf16[8,256,1024]{1,2,0:T(8,128)(2,1)} %stack.2), calls=%async_computation | async-start | bytes 8388608 | tf_op jit(solution)/shard_map/all_to_all | solution.py:19
  51.6 286.3 %reduce-scatter.2.cloned.1.call-start = ((), (), s32[]{:S(2)}) async-start(), calls=%async_computation.3 | async-start | bytes 9437184 | tf_op jit(solution)/shard_map/reduce_scatter | solution.py:133
  150.3 1.9 copy-start.3
  154.0 4.1 %copy-start.4 = (bf16[256,8192]{0,1:T(8,128)(2,1)S(1)}, bf16[256,8192]{0,1:T(8,128)(2,1)}, u32[]{:S(2)}) copy-start(bf16[256,8192]{0,1:T(8,128)(2,1)} %copy-done.3) | copy-start | bytes 12582916
  174.5 4.9 %copy-start.5 = (bf16[2,8,128,2,1,128]{5,2,1,0,3,4:T(8,128)(2,1)S(1)}, bf16[2,8,128,2,1,128]{5,2,1,0,3,4:T(8,128)(2,1)}, u32[]{:S(2)}) copy-start(bf16[2,8,128,2,1,128]{5,2,1,0,3,4:T(8,128)(2,1)} %copy.93) | copy-start | bytes 3145732
  177.3 5.4 %slice-start = ((s8[16777216]{0:T(1024)(128)(4,1)}), s8[4194304]{0:T(1024)(128)(4,1)S(1)}, s32[]{:S(2)}) async-start(s8[16777216]{0:T(1024)(128)(4,1)} %bitcast.109), calls=%async_computation.5 | async-start | bytes 8388608
  179.5 2.5 copy-start.6
  179.5 3.3 slice-start.1
  179.5 3.4 slice-start.2
  179.5 4.6 %slice-start.3 = ((s8[16777216]{0:T(1024)(128)(4,1)}), s8[4194304]{0:T(1024)(128)(4,1)S(1)}, s32[]{:S(2)}) async-start(s8[16777216]{0:T(1024)(128)(4,1)} %bitcast.109), calls=%async_computation.8 | async-start | bytes 8388608
  184.1 167.1 %copy-start.1 = (bf16[8192,128]{1,0:T(8,128)(2,1)S(1)}, bf16[8192,128]{1,0:T(8,128)(2,1)}, u32[]{:S(2)}) copy-start(bf16[8192,128]{1,0:T(8,128)(2,1)} %param.14) | copy-start | bytes 6291460
  190.8 149.2 %copy-start.8 = (s32[4]{0:T(128)S(1)}, s32[4]{0:T(128)}, u32[]{:S(2)}) copy-start(s32[4]{0:T(128)} %param.19) | copy-start | bytes 52
  190.9 157.5 %all-gather.2.cloned.1.call-start = ((), (), s32[]{:S(2)}) async-start(), calls=%async_computation.4 | async-start | bytes 1572864 | tf_op jit(solution)/shard_map/all_gather | solution.py:173
Sparse Core Ops, SparseCore 0:
  191.0 146.9 reduce-scatter.1
  340.2 8.0 all-gather.1
